TPU v7x, 256 devices: a whole 4x4x8 slice. The times are simulated.
256 devices in a mesh: tm: 8 (over x_hi, y), chan: 32 (over z, x_lo, core).
Axes of the slice: x: 4 (x_hi: 2, x_lo: 2; x = x_hi * 2 + x_lo), y: 4, z: 8, core: 2. Of those that a mesh axis runs over, the one named last changes fastest.
Arguments:
- vis: bfloat16 [512, 1024, 512], P('tm', 'chan'), may hold values from -6 to 6
- beam: bfloat16 [16, 1024, 2, 64, 256], P('tm', 'chan'), may hold values from -0.25 to 0.25
- fg_cov: float32 [1024, 1024], replicated, may hold values from 0 to 30, as said below
- flags: int32 [1024], replicated, may hold values 0 or 1
- m_modes: int32 [16], replicated, may hold values from 0 to 255, as said below
Outputs:
- filled: float32 [16, 2, 64, 1024], P('tm', None, None, 'chan')
Inputs may be any that keep to these rules, and one draw needn't show every extreme that they name: `m_modes`: m numbers of the window; entries may repeat. `fg_cov`: symmetric and positive definite.
All inputs are finite; a program needn't handle non-finite values.
Results may differ from a plain program's by a relative error of at most 0.0085.
Values sent between devices are 32-bit elements; how exact they have to be, the bound alone decides.
A program may use at most 64 MiB of HBM per device.

v0:
```python
import math
import jax
import jax.numpy as jnp
from jax import lax
from jax.sharding import PartitionSpec as P

ITERS = 10
EPS = 1e-06


def conjugate_fill(rows, good, apply_cov, curv_total, norm_total):

    def operator(vec):
        return vec + good * apply_cov(good * vec)

    start = good * rows
    norm_now = norm_total(start * start)[:, None]

    def advance(step, carry):
        sol, resid, direc, norm_now = carry
        image = operator(direc)
        alpha = norm_now / (curv_total(direc * image)[:, None] + EPS)
        sol = sol + alpha * direc
        resid = resid - alpha * image
        norm_next = norm_total(resid * resid)[:, None]
        direc = resid + norm_next / (norm_now + EPS) * direc
        return (sol, resid, direc, norm_next)

    sol, resid, direc, norm_now = lax.fori_loop(
        0, ITERS, advance, (jnp.zeros_like(rows), start, start, norm_now)
    )
    signal = apply_cov(good * sol)
    return good * rows + (1.0 - good) * signal


def per_device(vis, beam, fg_cov, flags, m_modes):
    t_dev = vis.shape[0]
    f_dev = vis.shape[1]
    width = vis.shape[2]
    half_width = width // 2
    n_time = t_dev * lax.axis_size("tm")
    m_dev = m_modes.shape[0] // lax.axis_size("tm")
    times = lax.axis_index("tm") * t_dev + jnp.arange(t_dev, dtype=jnp.int32)
    flat = vis.reshape(t_dev, f_dev * width)
    scale = 1.0 / math.sqrt(n_time)
    index = m_modes[:, None] * times[None, :] % n_time
    angle = 2.0 * math.pi / n_time * index.astype(jnp.float32)
    tables = jnp.concatenate([jnp.cos(angle), jnp.sin(angle)], axis=0).astype(jnp.bfloat16)
    prod = jnp.dot(tables, flat, preferred_element_type=jnp.float32).reshape(
        2, m_dev * lax.axis_size("tm"), f_dev, width
    )
    cos_part = prod[0]
    sin_part = prod[1]
    real_part = (cos_part[..., :half_width] + sin_part[..., half_width:]) * scale
    imag_part = (cos_part[..., half_width:] - sin_part[..., :half_width]) * scale
    mvis = lax.psum_scatter(
        jnp.concatenate([real_part, imag_part], axis=-1), "tm", scatter_dimension=0, tiled=True
    ).astype(jnp.bfloat16)
    prods = jnp.einsum(
        "mfpln,mfqn->mpqlf",
        beam,
        mvis.reshape(m_dev, f_dev, 2, half_width),
        preferred_element_type=jnp.float32,
    )
    coeffs = jnp.stack([prods[:, 0, 0] - prods[:, 1, 1], prods[:, 1, 0] + prods[:, 0, 1]], axis=1)
    degrees = coeffs.shape[2]
    good = (1 - flags).astype(jnp.float32)
    offset = lax.axis_index("chan") * f_dev
    good_here = lax.dynamic_slice_in_dim(good, offset, f_dev)
    cov_rows = lax.dynamic_slice_in_dim(fg_cov, offset, f_dev, 0)
    rows = coeffs.reshape(-1, f_dev)

    def spread_cov(vec):
        return lax.dot_general(
            lax.all_gather(vec, "chan", axis=1, tiled=True),
            cov_rows,
            (((1,), (1,)), ((), ())),
            precision=lax.Precision.HIGHEST,
            preferred_element_type=jnp.float32,
        )

    def curv_sum(values):
        return lax.psum(jnp.sum(values, axis=1), "chan")

    def norm_sum(values):
        return lax.psum(jnp.sum(values, axis=1), "chan")

    result = conjugate_fill(rows, good_here, spread_cov, curv_sum, norm_sum).reshape(
        m_dev, 2, degrees, f_dev
    )
    return result


def solution(mesh):
    placed = (P("tm", "chan", None), P("tm", "chan", None, None, None), P(), P(), P())
    return jax.shard_map(
        per_device,
        mesh=mesh,
        in_specs=placed,
        out_specs=P("tm", None, None, "chan"),
        check_vma=False,
    )
```

profile of v0, /device:TPU:1, one launch (start us, length us, event | category | flops | bytes accessed | tf_op | source)
XLA Modules:
  0.0 1975.6 jit_solution(2381233454197458835)
XLA Ops:
  13.7 78.5 %reduce-scatter.2.cloned.1.call-done = f32[2,32,512]{2,1,0:T(8,128)} async-done(((f32[16,32,512]{2,1,0:T(8,128)}), f32[2,32,512]{2,1,0:T(8,128)}) %reduce-scatter.2.cloned.1.call-update) | async-done | bytes 131088 | tf_op jit(solution)/shard_map/reduce_scatter | solution.py:56
  97.7 54.9 %psum.21 = f32[256,1]{0,1:T(1,128)S(1)} all-reduce(f32[256,1]{0,1:T(1,128)S(1)} %broadcast_in_dim.7), channel_id=1, replica_groups=mesh['tm'=8,'chan'=32] {'chan'}, use_global_device_ids=true, to_apply=%region_2.3 | all-reduce | flops 256 | bytes 2048 | tf_op jit(solution)/shard_map/psum | solution.py:86
  152.6 1748.1 %while.17 = (s32[]{:T(128)}, f32[256,32]{0,1:T(8,128)S(1)}, f32[256,32]{0,1:T(8,128)S(1)}, f32[256,32]{0,1:T(8,128)S(1)}, f32[256,1]{0,1:T(1,128)S(1)}, /*index=...) while((s32[]{:T(128)}, f32[256,32]{0,1:T(8,128)S(1)}, f32[256,32]{0,1:T(8,128)S(1)}, ...), condition=%wide.region_8.9_spmd.clone, body=%wide.region_3.8_spmd.clone.sunk | while | flops 100779008 | bytes 4836751 | solution.py:29
  153.4 64.9 %all-gather.5.cloned.1.call-done = f32[256,1024]{0,1:T(8,128)} async-done(((f32[256,32]{0,1:T(8,128)}), f32[256,1024]{0,1:T(8,128)}) %all-gather.5.cloned.1.call-update) | async-done | bytes 1048592 | tf_op jit(solution)/shard_map/while/body/eval_jaxpr/all_gather | solution.py:75
  272.9 54.6 %psum.27 = f32[256,1]{0,1:T(1,128)S(1)} all-reduce(f32[256,1]{0,1:T(1,128)S(1)} %bitcast.53), channel_id=1, replica_groups=mesh['tm'=8,'chan'=32] {'chan'}, use_global_device_ids=true, to_apply=%region_7.7 | all-reduce | flops 256 | bytes 2048 | tf_op jit(solution)/shard_map/while/body/eval_jaxpr/psum | solution.py:86
  328.3 64.9 %all-gather.5.cloned.1.call-done = f32[256,1024]{0,1:T(8,128)} async-done(((f32[256,32]{0,1:T(8,128)}), f32[256,1024]{0,1:T(8,128)}) %all-gather.5.cloned.1.call-update) | async-done | bytes 1048592 | tf_op jit(solution)/shard_map/while/body/eval_jaxpr/all_gather | solution.py:75
  447.8 54.6 %psum.27 = f32[256,1]{0,1:T(1,128)S(1)} all-reduce(f32[256,1]{0,1:T(1,128)S(1)} %bitcast.53), channel_id=1, replica_groups=mesh['tm'=8,'chan'=32] {'chan'}, use_global_device_ids=true, to_apply=%region_7.7 | all-reduce | flops 256 | bytes 2048 | tf_op jit(solution)/shard_map/while/body/eval_jaxpr/psum | solution.py:86
  503.2 64.6 %all-gather.5.cloned.1.call-done = f32[256,1024]{0,1:T(8,128)} async-done(((f32[256,32]{0,1:T(8,128)}), f32[256,1024]{0,1:T(8,128)}) %all-gather.5.cloned.1.call-update) | async-done | bytes 1048592 | tf_op jit(solution)/shard_map/while/body/eval_jaxpr/all_gather | solution.py:75
  622.4 54.6 %psum.27 = f32[256,1]{0,1:T(1,128)S(1)} all-reduce(f32[256,1]{0,1:T(1,128)S(1)} %bitcast.53), channel_id=1, replica_groups=mesh['tm'=8,'chan'=32] {'chan'}, use_global_device_ids=true, to_apply=%region_7.7 | all-reduce | flops 256 | bytes 2048 | tf_op jit(solution)/shard_map/while/body/eval_jaxpr/psum | solution.py:86
  677.9 64.6 %all-gather.5.cloned.1.call-done = f32[256,1024]{0,1:T(8,128)} async-done(((f32[256,32]{0,1:T(8,128)}), f32[256,1024]{0,1:T(8,128)}) %all-gather.5.cloned.1.call-update) | async-done | bytes 1048592 | tf_op jit(solution)/shard_map/while/body/eval_jaxpr/all_gather | solution.py:75
  797.1 54.6 %psum.27 = f32[256,1]{0,1:T(1,128)S(1)} all-reduce(f32[256,1]{0,1:T(1,128)S(1)} %bitcast.53), channel_id=1, replica_groups=mesh['tm'=8,'chan'=32] {'chan'}, use_global_device_ids=true, to_apply=%region_7.7 | all-reduce | flops 256 | bytes 2048 | tf_op jit(solution)/shard_map/while/body/eval_jaxpr/psum | solution.py:86
  852.5 64.6 %all-gather.5.cloned.1.call-done = f32[256,1024]{0,1:T(8,128)} async-done(((f32[256,32]{0,1:T(8,128)}), f32[256,1024]{0,1:T(8,128)}) %all-gather.5.cloned.1.call-update) | async-done | bytes 1048592 | tf_op jit(solution)/shard_map/while/body/eval_jaxpr/all_gather | solution.py:75
  971.7 54.6 %psum.27 = f32[256,1]{0,1:T(1,128)S(1)} all-reduce(f32[256,1]{0,1:T(1,128)S(1)} %bitcast.53), channel_id=1, replica_groups=mesh['tm'=8,'chan'=32] {'chan'}, use_global_device_ids=true, to_apply=%region_7.7 | all-reduce | flops 256 | bytes 2048 | tf_op jit(solution)/shard_map/while/body/eval_jaxpr/psum | solution.py:86
  1027.1 65.0 %all-gather.5.cloned.1.call-done = f32[256,1024]{0,1:T(8,128)} async-done(((f32[256,32]{0,1:T(8,128)}), f32[256,1024]{0,1:T(8,128)}) %all-gather.5.cloned.1.call-update) | async-done | bytes 1048592 | tf_op jit(solution)/shard_map/while/body/eval_jaxpr/all_gather | solution.py:75
  1146.6 54.6 %psum.27 = f32[256,1]{0,1:T(1,128)S(1)} all-reduce(f32[256,1]{0,1:T(1,128)S(1)} %bitcast.53), channel_id=1, replica_groups=mesh['tm'=8,'chan'=32] {'chan'}, use_global_device_ids=true, to_apply=%region_7.7 | all-reduce | flops 256 | bytes 2048 | tf_op jit(solution)/shard_map/while/body/eval_jaxpr/psum | solution.py:86
  1202.1 65.0 %all-gather.5.cloned.1.call-done = f32[256,1024]{0,1:T(8,128)} async-done(((f32[256,32]{0,1:T(8,128)}), f32[256,1024]{0,1:T(8,128)}) %all-gather.5.cloned.1.call-update) | async-done | bytes 1048592 | tf_op jit(solution)/shard_map/while/body/eval_jaxpr/all_gather | solution.py:75
  1321.6 54.6 %psum.27 = f32[256,1]{0,1:T(1,128)S(1)} all-reduce(f32[256,1]{0,1:T(1,128)S(1)} %bitcast.53), channel_id=1, replica_groups=mesh['tm'=8,'chan'=32] {'chan'}, use_global_device_ids=true, to_apply=%region_7.7 | all-reduce | flops 256 | bytes 2048 | tf_op jit(solution)/shard_map/while/body/eval_jaxpr/psum | solution.py:86
  1377.0 64.9 %all-gather.5.cloned.1.call-done = f32[256,1024]{0,1:T(8,128)} async-done(((f32[256,32]{0,1:T(8,128)}), f32[256,1024]{0,1:T(8,128)}) %all-gather.5.cloned.1.call-update) | async-done | bytes 1048592 | tf_op jit(solution)/shard_map/while/body/eval_jaxpr/all_gather | solution.py:75
  1496.5 54.6 %psum.27 = f32[256,1]{0,1:T(1,128)S(1)} all-reduce(f32[256,1]{0,1:T(1,128)S(1)} %bitcast.53), channel_id=1, replica_groups=mesh['tm'=8,'chan'=32] {'chan'}, use_global_device_ids=true, to_apply=%region_7.7 | all-reduce | flops 256 | bytes 2048 | tf_op jit(solution)/shard_map/while/body/eval_jaxpr/psum | solution.py:86
  1552.0 64.6 %all-gather.5.cloned.1.call-done = f32[256,1024]{0,1:T(8,128)} async-done(((f32[256,32]{0,1:T(8,128)}), f32[256,1024]{0,1:T(8,128)}) %all-gather.5.cloned.1.call-update) | async-done | bytes 1048592 | tf_op jit(solution)/shard_map/while/body/eval_jaxpr/all_gather | solution.py:75
  1671.2 54.6 %psum.27 = f32[256,1]{0,1:T(1,128)S(1)} all-reduce(f32[256,1]{0,1:T(1,128)S(1)} %bitcast.53), channel_id=1, replica_groups=mesh['tm'=8,'chan'=32] {'chan'}, use_global_device_ids=true, to_apply=%region_7.7 | all-reduce | flops 256 | bytes 2048 | tf_op jit(solution)/shard_map/while/body/eval_jaxpr/psum | solution.py:86
  1726.6 64.9 %all-gather.5.cloned.1.call-done = f32[256,1024]{0,1:T(8,128)} async-done(((f32[256,32]{0,1:T(8,128)}), f32[256,1024]{0,1:T(8,128)}) %all-gather.5.cloned.1.call-update) | async-done | bytes 1048592 | tf_op jit(solution)/shard_map/while/body/eval_jaxpr/all_gather | solution.py:75
  1846.1 54.6 %psum.27 = f32[256,1]{0,1:T(1,128)S(1)} all-reduce(f32[256,1]{0,1:T(1,128)S(1)} %bitcast.53), channel_id=1, replica_groups=mesh['tm'=8,'chan'=32] {'chan'}, use_global_device_ids=true, to_apply=%region_7.7 | all-reduce | flops 256 | bytes 2048 | tf_op jit(solution)/shard_map/while/body/eval_jaxpr/psum | solution.py:86
  1901.5 64.6 %all-gather.3.cloned.1.call-done = f32[256,1024]{0,1:T(8,128)} async-done(((f32[256,32]{0,1:T(8,128)}), f32[256,1024]{0,1:T(8,128)}) %all-gather.3.cloned.1.call-update) | async-done | bytes 1048592 | tf_op jit(solution)/shard_map/all_gather | solution.py:75
  (148 shorter events, 569.2 us)
Async XLA Ops:
  6.5 85.7 %reduce-scatter.2.cloned.1.call-start = ((), (), s32[]{:S(2)}) async-start(), calls=%async_computation.1 | async-start | bytes 1179648 | tf_op jit(solution)/shard_map/reduce_scatter | solution.py:56
  6.5 2.9 copy-start.1
  11.5 1.2 copy-start
  152.6 65.7 %all-gather.5.cloned.1.call-start = ((), (), s32[]{:S(2)}) async-start(), calls=%async_computation.3 | async-start | bytes 1081344 | tf_op jit(solution)/shard_map/while/body/eval_jaxpr/all_gather | solution.py:75
  327.5 65.7 %all-gather.5.cloned.1.call-start = ((), (), s32[]{:S(2)}) async-start(), calls=%async_computation.3 | async-start | bytes 1081344 | tf_op jit(solution)/shard_map/while/body/eval_jaxpr/all_gather | solution.py:75
  502.5 65.4 %all-gather.5.cloned.1.call-start = ((), (), s32[]{:S(2)}) async-start(), calls=%async_computation.3 | async-start | bytes 1081344 | tf_op jit(solution)/shard_map/while/body/eval_jaxpr/all_gather | solution.py:75
  677.1 65.4 %all-gather.5.cloned.1.call-start = ((), (), s32[]{:S(2)}) async-start(), calls=%async_computation.3 | async-start | bytes 1081344 | tf_op jit(solution)/shard_map/while/body/eval_jaxpr/all_gather | solution.py:75
  851.7 65.4 %all-gather.5.cloned.1.call-start = ((), (), s32[]{:S(2)}) async-start(), calls=%async_computation.3 | async-start | bytes 1081344 | tf_op jit(solution)/shard_map/while/body/eval_jaxpr/all_gather | solution.py:75
  1026.4 65.7 %all-gather.5.cloned.1.call-start = ((), (), s32[]{:S(2)}) async-start(), calls=%async_computation.3 | async-start | bytes 1081344 | tf_op jit(solution)/shard_map/while/body/eval_jaxpr/all_gather | solution.py:75
  1201.3 65.7 %all-gather.5.cloned.1.call-start = ((), (), s32[]{:S(2)}) async-start(), calls=%async_computation.3 | async-start | bytes 1081344 | tf_op jit(solution)/shard_map/while/body/eval_jaxpr/all_gather | solution.py:75
  1376.2 65.7 %all-gather.5.cloned.1.call-start = ((), (), s32[]{:S(2)}) async-start(), calls=%async_computation.3 | async-start | bytes 1081344 | tf_op jit(solution)/shard_map/while/body/eval_jaxpr/all_gather | solution.py:75
  1551.2 65.4 %all-gather.5.cloned.1.call-start = ((), (), s32[]{:S(2)}) async-start(), calls=%async_computation.3 | async-start | bytes 1081344 | tf_op jit(solution)/shard_map/while/body/eval_jaxpr/all_gather | solution.py:75
  1725.8 65.7 %all-gather.5.cloned.1.call-start = ((), (), s32[]{:S(2)}) async-start(), calls=%async_computation.3 | async-start | bytes 1081344 | tf_op jit(solution)/shard_map/while/body/eval_jaxpr/all_gather | solution.py:75
  1900.8 65.4 %all-gather.3.cloned.1.call-start = ((), (), s32[]{:S(2)}) async-start(), calls=%async_computation.2 | async-start | bytes 1081344 | tf_op jit(solution)/shard_map/all_gather | solution.py:75
Sparse Core Ops, SparseCore 0:
  12.8 79.3 reduce-scatter.1
  155.3 62.9 all-gather.4
  330.2 63.0 all-gather.4
  504.8 63.0 all-gather.4
  679.4 63.0 all-gather.4
  854.1 63.0 all-gather.4
  1029.0 63.0 all-gather.4
  1204.0 63.0 all-gather.4
  1378.9 63.0 all-gather.4
  1553.6 63.0 all-gather.4
  1728.5 62.9 all-gather.4
  1903.1 63.0 all-gather.2
where the time goes:
time: 1980 us
  blocking collectives  1130 us (57%)
  waiting for transfers between devices  792 us (40%)
  matrix products  25.1 us (1%)
    all_gather x11, waiting for transfers between devices, spread_cov(): lax.all_gather(vec, 'chan', axis=1, tiled=True)  713 us
    psum x11, blocking collectives, norm_sum(): return lax.psum(jnp.sum(values, axis=1), 'chan')  601 us
    psum x10, blocking collectives, curv_sum(): return lax.psum(jnp.sum(values, axis=1), 'chan')  526 us
    reduce_scatter x1, waiting for transfers between devices, per_device(): lax.psum_scatter(jnp.concatenate([real_part, imag_part], axis=-1), 'tm',...  78.5 us
  transfers between devices with their start and end apart: 12, of which 12 were waited for; matrix products, arithmetic and copies ran while one was open for 0% of the time, Pallas kernels for 0%

commit v1 on v0

--- a/solution.py
+++ b/solution.py
@@ -71,8 +71,11 @@
     rows = coeffs.reshape(-1, f_dev)
 
     def spread_cov(vec):
+        prepare_packet = lambda local_x: jnp.concatenate(
+            lax.all_to_all(jnp.stack([local_x] * lax.psum(1, "chan"), axis=0), "chan", 0, 0), axis=1
+        )
         return lax.dot_general(
-            lax.all_gather(vec, "chan", axis=1, tiled=True),
+            prepare_packet(vec),
             cov_rows,
             (((1,), (1,)), ((), ())),
             precision=lax.Precision.HIGHEST,

time: 1980 us -> 1620 us (0.82)
  waiting for transfers between devices: 792 us -> 359 us
  starting transfers between devices: 0.45 us -> 61.7 us
  blocking collectives: 1130 us -> 1150 us
    all_gather x11 -> x0, waiting for transfers between devices: 713 us -> none  [spread_cov(): lax.all_gather(vec, 'chan', axis=1, tiled=True)]
    all_to_all x0 -> x10, waiting for transfers between devices: none -> 281 us  [spread_cov(): lax.all_to_all(jnp.stack([local_x] * lax.psum(1, 'chan'), axis=0), 'chan'...]
    all_to_all x0 -> x10, starting transfers between devices: none -> 61.7 us  [spread_cov(): lax.all_to_all(jnp.stack([local_x] * lax.psum(1, 'chan'), axis=0), 'chan'...]
    all_to_all x0 -> x1, blocking collectives: none -> 33.9 us  [spread_cov(): lax.all_to_all(jnp.stack([local_x] * lax.psum(1, 'chan'), axis=0), 'chan'...]
  transfers between devices with their start and end apart: 12 -> 11, of which waited for: 12 -> 11; matrix products, arithmetic and copies ran while one was open for 0% -> 0% of each run, Pallas kernels for 0% -> 0%
where the time goes in v1:
time: 1620 us
  blocking collectives  1150 us (71%)
  waiting for transfers between devices  359 us (22%)
  starting transfers between devices  61.7 us (4%)
  local copies, waits for them, and re-layouts  17.4 us (1%)
    psum x11, blocking collectives, norm_sum(): return lax.psum(jnp.sum(values, axis=1), 'chan')  585 us
    psum x10, blocking collectives, curv_sum(): return lax.psum(jnp.sum(values, axis=1), 'chan')  531 us
    all_to_all x10, waiting for transfers between devices, spread_cov(): lax.all_to_all(jnp.stack([local_x] * lax.psum(1, 'chan'), axis=0), 'chan'...  281 us
    reduce_scatter x1, waiting for transfers between devices, per_device(): lax.psum_scatter(jnp.concatenate([real_part, imag_part], axis=-1), 'tm',...  78.6 us
    all_to_all x10, starting transfers between devices, spread_cov(): lax.all_to_all(jnp.stack([local_x] * lax.psum(1, 'chan'), axis=0), 'chan'...  61.7 us
    all_to_all x1, blocking collectives, spread_cov(): lax.all_to_all(jnp.stack([local_x] * lax.psum(1, 'chan'), axis=0), 'chan'...  33.9 us
  transfers between devices with their start and end apart: 11, of which 11 were waited for; matrix products, arithmetic and copies ran while one was open for 0% of the time, Pallas kernels for 0%

profile of v1, /device:TPU:1, one launch (start us, length us, event | category | flops | bytes accessed | tf_op | source)
XLA Modules:
  0.0 1617.8 jit_solution(14337200872379805944)
XLA Ops:
  13.7 78.6 %reduce-scatter.2.cloned.1.call-done = f32[2,32,512]{2,1,0:T(8,128)} async-done(((f32[16,32,512]{2,1,0:T(8,128)}), f32[2,32,512]{2,1,0:T(8,128)}) %reduce-scatter.2.cloned.1.call-update) | async-done | bytes 131088 | tf_op jit(solution)/shard_map/reduce_scatter | solution.py:56
  97.7 54.9 %psum.21 = f32[256,1]{0,1:T(1,128)S(1)} all-reduce(f32[256,1]{0,1:T(1,128)S(1)} %broadcast_in_dim.7), channel_id=1, replica_groups=mesh['tm'=8,'chan'=32] {'chan'}, use_global_device_ids=true, to_apply=%region_2.3 | all-reduce | flops 256 | bytes 2048 | tf_op jit(solution)/shard_map/psum | solution.py:89
  152.6 1422.9 %while.17 = (s32[]{:T(128)}, f32[256,32]{0,1:T(8,128)S(1)}, f32[256,32]{0,1:T(8,128)S(1)}, f32[256,32]{0,1:T(8,128)S(1)}, f32[256,1]{0,1:T(1,128)S(1)}, /*index=...) while((s32[]{:T(128)}, f32[256,32]{0,1:T(8,128)S(1)}, f32[256,32]{0,1:T(8,128)S(1)}, ...), condition=%wide.region_8.9_spmd.clone, body=%wide.region_3.8_spmd.clone.sunk | while | flops 100779008 | bytes 5819783 | solution.py:29
  190.4 53.1 %psum.26 = f32[256]{0:T(256)S(1)} all-reduce(f32[256]{0:T(256)S(1)} %get-tuple-element.150), channel_id=1, replica_groups=mesh['tm'=8,'chan'=32] {'chan'}, use_global_device_ids=true, to_apply=%region_5.5 | all-reduce | flops 256 | bytes 2048 | tf_op jit(solution)/shard_map/while/body/eval_jaxpr/psum | solution.py:86
  243.5 53.0 %psum.27 = f32[256,1]{0,1:T(1,128)S(1)} all-reduce(f32[256,1]{0,1:T(1,128)S(1)} %bitcast.63), channel_id=1, replica_groups=mesh['tm'=8,'chan'=32] {'chan'}, use_global_device_ids=true, to_apply=%region_7.7 | all-reduce | flops 256 | bytes 2048 | tf_op jit(solution)/shard_map/while/body/eval_jaxpr/psum | solution.py:89
  332.5 53.1 %psum.26 = f32[256]{0:T(256)S(1)} all-reduce(f32[256]{0:T(256)S(1)} %get-tuple-element.150), channel_id=1, replica_groups=mesh['tm'=8,'chan'=32] {'chan'}, use_global_device_ids=true, to_apply=%region_5.5 | all-reduce | flops 256 | bytes 2048 | tf_op jit(solution)/shard_map/while/body/eval_jaxpr/psum | solution.py:86
  385.6 53.0 %psum.27 = f32[256,1]{0,1:T(1,128)S(1)} all-reduce(f32[256,1]{0,1:T(1,128)S(1)} %bitcast.63), channel_id=1, replica_groups=mesh['tm'=8,'chan'=32] {'chan'}, use_global_device_ids=true, to_apply=%region_7.7 | all-reduce | flops 256 | bytes 2048 | tf_op jit(solution)/shard_map/while/body/eval_jaxpr/psum | solution.py:89
  474.6 53.1 %psum.26 = f32[256]{0:T(256)S(1)} all-reduce(f32[256]{0:T(256)S(1)} %get-tuple-element.150), channel_id=1, replica_groups=mesh['tm'=8,'chan'=32] {'chan'}, use_global_device_ids=true, to_apply=%region_5.5 | all-reduce | flops 256 | bytes 2048 | tf_op jit(solution)/shard_map/while/body/eval_jaxpr/psum | solution.py:86
  527.7 53.0 %psum.27 = f32[256,1]{0,1:T(1,128)S(1)} all-reduce(f32[256,1]{0,1:T(1,128)S(1)} %bitcast.63), channel_id=1, replica_groups=mesh['tm'=8,'chan'=32] {'chan'}, use_global_device_ids=true, to_apply=%region_7.7 | all-reduce | flops 256 | bytes 2048 | tf_op jit(solution)/shard_map/while/body/eval_jaxpr/psum | solution.py:89
  616.7 53.1 %psum.26 = f32[256]{0:T(256)S(1)} all-reduce(f32[256]{0:T(256)S(1)} %get-tuple-element.150), channel_id=1, replica_groups=mesh['tm'=8,'chan'=32] {'chan'}, use_global_device_ids=true, to_apply=%region_5.5 | all-reduce | flops 256 | bytes 2048 | tf_op jit(solution)/shard_map/while/body/eval_jaxpr/psum | solution.py:86
  669.9 53.0 %psum.27 = f32[256,1]{0,1:T(1,128)S(1)} all-reduce(f32[256,1]{0,1:T(1,128)S(1)} %bitcast.63), channel_id=1, replica_groups=mesh['tm'=8,'chan'=32] {'chan'}, use_global_device_ids=true, to_apply=%region_7.7 | all-reduce | flops 256 | bytes 2048 | tf_op jit(solution)/shard_map/while/body/eval_jaxpr/psum | solution.py:89
  758.8 53.1 %psum.26 = f32[256]{0:T(256)S(1)} all-reduce(f32[256]{0:T(256)S(1)} %get-tuple-element.150), channel_id=1, replica_groups=mesh['tm'=8,'chan'=32] {'chan'}, use_global_device_ids=true, to_apply=%region_5.5 | all-reduce | flops 256 | bytes 2048 | tf_op jit(solution)/shard_map/while/body/eval_jaxpr/psum | solution.py:86
  812.0 53.0 %psum.27 = f32[256,1]{0,1:T(1,128)S(1)} all-reduce(f32[256,1]{0,1:T(1,128)S(1)} %bitcast.63), channel_id=1, replica_groups=mesh['tm'=8,'chan'=32] {'chan'}, use_global_device_ids=true, to_apply=%region_7.7 | all-reduce | flops 256 | bytes 2048 | tf_op jit(solution)/shard_map/while/body/eval_jaxpr/psum | solution.py:89
  900.9 53.1 %psum.26 = f32[256]{0:T(256)S(1)} all-reduce(f32[256]{0:T(256)S(1)} %get-tuple-element.150), channel_id=1, replica_groups=mesh['tm'=8,'chan'=32] {'chan'}, use_global_device_ids=true, to_apply=%region_5.5 | all-reduce | flops 256 | bytes 2048 | tf_op jit(solution)/shard_map/while/body/eval_jaxpr/psum | solution.py:86
  954.1 53.0 %psum.27 = f32[256,1]{0,1:T(1,128)S(1)} all-reduce(f32[256,1]{0,1:T(1,128)S(1)} %bitcast.63), channel_id=1, replica_groups=mesh['tm'=8,'chan'=32] {'chan'}, use_global_device_ids=true, to_apply=%region_7.7 | all-reduce | flops 256 | bytes 2048 | tf_op jit(solution)/shard_map/while/body/eval_jaxpr/psum | solution.py:89
  1043.0 53.1 %psum.26 = f32[256]{0:T(256)S(1)} all-reduce(f32[256]{0:T(256)S(1)} %get-tuple-element.150), channel_id=1, replica_groups=mesh['tm'=8,'chan'=32] {'chan'}, use_global_device_ids=true, to_apply=%region_5.5 | all-reduce | flops 256 | bytes 2048 | tf_op jit(solution)/shard_map/while/body/eval_jaxpr/psum | solution.py:86
  1096.2 53.0 %psum.27 = f32[256,1]{0,1:T(1,128)S(1)} all-reduce(f32[256,1]{0,1:T(1,128)S(1)} %bitcast.63), channel_id=1, replica_groups=mesh['tm'=8,'chan'=32] {'chan'}, use_global_device_ids=true, to_apply=%region_7.7 | all-reduce | flops 256 | bytes 2048 | tf_op jit(solution)/shard_map/while/body/eval_jaxpr/psum | solution.py:89
  1185.2 53.1 %psum.26 = f32[256]{0:T(256)S(1)} all-reduce(f32[256]{0:T(256)S(1)} %get-tuple-element.150), channel_id=1, replica_groups=mesh['tm'=8,'chan'=32] {'chan'}, use_global_device_ids=true, to_apply=%region_5.5 | all-reduce | flops 256 | bytes 2048 | tf_op jit(solution)/shard_map/while/body/eval_jaxpr/psum | solution.py:86
  1238.3 53.0 %psum.27 = f32[256,1]{0,1:T(1,128)S(1)} all-reduce(f32[256,1]{0,1:T(1,128)S(1)} %bitcast.63), channel_id=1, replica_groups=mesh['tm'=8,'chan'=32] {'chan'}, use_global_device_ids=true, to_apply=%region_7.7 | all-reduce | flops 256 | bytes 2048 | tf_op jit(solution)/shard_map/while/body/eval_jaxpr/psum | solution.py:89
  1327.3 53.1 %psum.26 = f32[256]{0:T(256)S(1)} all-reduce(f32[256]{0:T(256)S(1)} %get-tuple-element.150), channel_id=1, replica_groups=mesh['tm'=8,'chan'=32] {'chan'}, use_global_device_ids=true, to_apply=%region_5.5 | all-reduce | flops 256 | bytes 2048 | tf_op jit(solution)/shard_map/while/body/eval_jaxpr/psum | solution.py:86
  1380.4 53.0 %psum.27 = f32[256,1]{0,1:T(1,128)S(1)} all-reduce(f32[256,1]{0,1:T(1,128)S(1)} %bitcast.63), channel_id=1, replica_groups=mesh['tm'=8,'chan'=32] {'chan'}, use_global_device_ids=true, to_apply=%region_7.7 | all-reduce | flops 256 | bytes 2048 | tf_op jit(solution)/shard_map/while/body/eval_jaxpr/psum | solution.py:89
  1469.4 53.1 %psum.26 = f32[256]{0:T(256)S(1)} all-reduce(f32[256]{0:T(256)S(1)} %get-tuple-element.150), channel_id=1, replica_groups=mesh['tm'=8,'chan'=32] {'chan'}, use_global_device_ids=true, to_apply=%region_5.5 | all-reduce | flops 256 | bytes 2048 | tf_op jit(solution)/shard_map/while/body/eval_jaxpr/psum | solution.py:86
  1522.5 53.0 %psum.27 = f32[256,1]{0,1:T(1,128)S(1)} all-reduce(f32[256,1]{0,1:T(1,128)S(1)} %bitcast.63), channel_id=1, replica_groups=mesh['tm'=8,'chan'=32] {'chan'}, use_global_device_ids=true, to_apply=%region_7.7 | all-reduce | flops 256 | bytes 2048 | tf_op jit(solution)/shard_map/while/body/eval_jaxpr/psum | solution.py:89
  1575.7 33.9 %all_to_all.12 = f32[32,256,32]{1,2,0:T(8,128)S(1)} all-to-all(f32[32,256,32]{1,2,0:T(8,128)S(1)} %stack.7), channel_id=1, replica_groups=mesh['tm'=8,'chan'=32] {'chan'}, dimensions={0} | all-to-all | bytes 2097152 | tf_op jit(solution)/shard_map/all_to_all | solution.py:75
  (147 shorter events, 375.7 us)
Async XLA Ops:
  6.5 85.7 %reduce-scatter.2.cloned.1.call-start = ((), (), s32[]{:S(2)}) async-start(), calls=%async_computation.3 | async-start | bytes 1179648 | tf_op jit(solution)/shard_map/reduce_scatter | solution.py:56
  6.5 2.9 copy-start.1
  11.5 1.2 copy-start
  153.8 35.9 %all-to-all-start = ((f32[32,256,32]{1,2,0:T(8,128)}), f32[32,256,32]{1,2,0:T(8,128)S(1)}, u32[]{:S(2)}, u32[]{:S(2)}) async-start(f32[32,256,32]{1,2,0:T(8,128)} %stack.10), calls=%async_computation | async-start | bytes 2097152 | tf_op jit(solution)/shard_map/while/body/eval_jaxpr/all_to_all | solution.py:75
  297.8 34.1 %all-to-all-start = ((f32[32,256,32]{1,2,0:T(8,128)}), f32[32,256,32]{1,2,0:T(8,128)S(1)}, u32[]{:S(2)}, u32[]{:S(2)}) async-start(f32[32,256,32]{1,2,0:T(8,128)} %stack.10), calls=%async_computation | async-start | bytes 2097152 | tf_op jit(solution)/shard_map/while/body/eval_jaxpr/all_to_all | solution.py:75
  439.9 34.1 %all-to-all-start = ((f32[32,256,32]{1,2,0:T(8,128)}), f32[32,256,32]{1,2,0:T(8,128)S(1)}, u32[]{:S(2)}, u32[]{:S(2)}) async-start(f32[32,256,32]{1,2,0:T(8,128)} %stack.10), calls=%async_computation | async-start | bytes 2097152 | tf_op jit(solution)/shard_map/while/body/eval_jaxpr/all_to_all | solution.py:75
  582.0 34.1 %all-to-all-start = ((f32[32,256,32]{1,2,0:T(8,128)}), f32[32,256,32]{1,2,0:T(8,128)S(1)}, u32[]{:S(2)}, u32[]{:S(2)}) async-start(f32[32,256,32]{1,2,0:T(8,128)} %stack.10), calls=%async_computation | async-start | bytes 2097152 | tf_op jit(solution)/shard_map/while/body/eval_jaxpr/all_to_all | solution.py:75
  724.1 34.1 %all-to-all-start = ((f32[32,256,32]{1,2,0:T(8,128)}), f32[32,256,32]{1,2,0:T(8,128)S(1)}, u32[]{:S(2)}, u32[]{:S(2)}) async-start(f32[32,256,32]{1,2,0:T(8,128)} %stack.10), calls=%async_computation | async-start | bytes 2097152 | tf_op jit(solution)/shard_map/while/body/eval_jaxpr/all_to_all | solution.py:75
  866.2 34.1 %all-to-all-start = ((f32[32,256,32]{1,2,0:T(8,128)}), f32[32,256,32]{1,2,0:T(8,128)S(1)}, u32[]{:S(2)}, u32[]{:S(2)}) async-start(f32[32,256,32]{1,2,0:T(8,128)} %stack.10), calls=%async_computation | async-start | bytes 2097152 | tf_op jit(solution)/shard_map/while/body/eval_jaxpr/all_to_all | solution.py:75
  1008.3 34.1 %all-to-all-start = ((f32[32,256,32]{1,2,0:T(8,128)}), f32[32,256,32]{1,2,0:T(8,128)S(1)}, u32[]{:S(2)}, u32[]{:S(2)}) async-start(f32[32,256,32]{1,2,0:T(8,128)} %stack.10), calls=%async_computation | async-start | bytes 2097152 | tf_op jit(solution)/shard_map/while/body/eval_jaxpr/all_to_all | solution.py:75
  1150.4 34.1 %all-to-all-start = ((f32[32,256,32]{1,2,0:T(8,128)}), f32[32,256,32]{1,2,0:T(8,128)S(1)}, u32[]{:S(2)}, u32[]{:S(2)}) async-start(f32[32,256,32]{1,2,0:T(8,128)} %stack.10), calls=%async_computation | async-start | bytes 2097152 | tf_op jit(solution)/shard_map/while/body/eval_jaxpr/all_to_all | solution.py:75
  1292.5 34.1 %all-to-all-start = ((f32[32,256,32]{1,2,0:T(8,128)}), f32[32,256,32]{1,2,0:T(8,128)S(1)}, u32[]{:S(2)}, u32[]{:S(2)}) async-start(f32[32,256,32]{1,2,0:T(8,128)} %stack.10), calls=%async_computation | async-start | bytes 2097152 | tf_op jit(solution)/shard_map/while/body/eval_jaxpr/all_to_all | solution.py:75
  1434.6 34.1 %all-to-all-start = ((f32[32,256,32]{1,2,0:T(8,128)}), f32[32,256,32]{1,2,0:T(8,128)S(1)}, u32[]{:S(2)}, u32[]{:S(2)}) async-start(f32[32,256,32]{1,2,0:T(8,128)} %stack.10), calls=%async_computation | async-start | bytes 2097152 | tf_op jit(solution)/shard_map/while/body/eval_jaxpr/all_to_all | solution.py:75
Sparse Core Ops, SparseCore 0:
  12.8 79.4 reduce-scatter.1
